TPU v7x, 256 devices: a whole 4x4x8 slice. The times are simulated.
256 devices in a mesh: pole: 8 (over y, x_lo), leaf: 32 (over x_hi, z, core).
Axes of the slice: x: 4 (x_hi: 2, x_lo: 2; x = x_hi * 2 + x_lo), y: 4, z: 8, core: 2. Of those that a mesh axis runs over, the one named last changes fastest.
Arguments:
- inverse_front: bfloat16 [8, 2, 8192, 8192], P('pole', None, 'leaf'), may hold values from -6 to 6
- factor_panel: bfloat16 [8, 8192, 512], P('pole', 'leaf'), may hold values from -0.0625 to 0.0625
- diag_inverse: bfloat16 [8, 256, 512], P('pole'), may hold values from -6 to 6
- pole_weight: float32 [8, 2], P('pole'), may hold values from -2.4 to 2.4
- structure: int32 [32], replicated, may hold values from 0 to 1, as said below
- block_owner: int32 [1024, 1], P('leaf'), may hold values from 0 to 31; in each aligned block of 32 rows (0 to 31, 32 to 63, ...) at most 2 rows name the same one
Outputs:
- owned_density: float32 [2048, 8, 256], P('leaf')
- diag_density: float32 [256, 256], replicated
Inputs may be any that keep to these rules, and one draw needn't show every extreme that they name: `structure`: exactly 16 entries are 1. `block_owner`: among the 32 blocks of one index of leaf no owner appears more than 2 times, and in some index's blocks one owner appears exactly 2 times.
All inputs are finite; a program needn't handle non-finite values.
Results may differ from a plain program's by a relative error of at most 0.0003.
Values may be sent and summed in bfloat16 or wider, within the bound.
No kernel may reach another device: no remote copies, remote signals or barrier semaphores. Data moves between devices by JAX's collectives and lax.ppermute only.
A program may use at most 64 MiB of HBM per device.

v0:
```python
import jax
import jax.numpy as jnp
from jax import lax
from jax.sharding import PartitionSpec as P


def kept_rows(structure, first_row, row_count, block_width):
    block_ids = jnp.arange(structure.shape[0], dtype=jnp.int32)
    which_block = (first_row + jnp.arange(row_count, dtype=jnp.int32)) // block_width
    matches = which_block[:, None] == block_ids[None, :]
    return jnp.sum(jnp.where(matches, structure[None, :], 0), axis=1).astype(jnp.float32)


def panel_product(columns, panel):
    return jnp.einsum("pcrk,pkn->pcrn", columns, panel, preferred_element_type=jnp.float32)


def body(inverse_front, factor_panel, diag_inverse, pole_weight, structure, block_owner):
    leaves = lax.axis_size("leaf")
    rows_here = inverse_front.shape[2]
    block_width = factor_panel.shape[2] // 2
    first_row = lax.axis_index("leaf") * rows_here
    panel_rows = lax.all_gather(factor_panel, "leaf", axis=1, tiled=True)
    row_count = panel_rows.shape[1]
    keep_piece = kept_rows(structure, jnp.int32(0), row_count, block_width).astype(jnp.bfloat16)
    masked = panel_rows * keep_piece[None, :, None]
    product = panel_product(inverse_front, masked)
    keep_here = kept_rows(structure, first_row, rows_here, block_width)[None, :, None]
    block_real = -(product[:, 0, :, :block_width] - product[:, 1, :, block_width:]) * keep_here
    block_imag = -(product[:, 0, :, block_width:] + product[:, 1, :, :block_width]) * keep_here
    weight_real = pole_weight[:, 0][:, None, None]
    weight_imag = pole_weight[:, 1][:, None, None]
    density_part = jnp.sum(weight_real * block_imag + weight_imag * block_real, axis=0)
    panel_kept = factor_panel.astype(jnp.float32) * keep_here
    panel_real = panel_kept[:, :, :block_width]
    panel_imag = panel_kept[:, :, block_width:]
    precise = lax.Precision.HIGHEST

    def transposed(left_side, right_side):
        return jnp.einsum("prk,prn->pkn", left_side, right_side, precision=precise)

    schur_real = transposed(panel_real, block_real) - transposed(panel_imag, block_imag)
    schur_imag = transposed(panel_real, block_imag) + transposed(panel_imag, block_real)
    diag_full = diag_inverse.astype(jnp.float32)
    schur_real, schur_imag = lax.psum((schur_real, schur_imag), "leaf")
    corner_real = diag_full[:, :, :block_width] - schur_real
    corner_imag = diag_full[:, :, block_width:] - schur_imag
    corner_terms = jnp.sum(weight_real * corner_imag + weight_imag * corner_real, axis=0)
    diag_density = lax.psum(corner_terms, "pole")
    blocks_mine = block_owner.shape[0]
    element_rows = rows_here // blocks_mine
    capacity = max(2, (2 * blocks_mine + leaves - 1) // leaves)
    owners = block_owner[:, 0]
    one_hot = (owners[:, None] == jnp.arange(leaves, dtype=jnp.int32)[None, :]).astype(jnp.int32)
    ranks = jnp.sum((jnp.cumsum(one_hot, axis=0) - one_hot) * one_hot, axis=1)
    slot_index = owners * capacity + ranks
    density_rows = lax.psum(density_part, "pole")
    column_count = density_rows.shape[1]
    element_blocks = density_rows.reshape(blocks_mine, element_rows, column_count)
    buffer_zero = jnp.zeros((leaves * capacity, element_rows, column_count), jnp.float32)
    owned_density = lax.all_to_all(
        buffer_zero.at[slot_index].set(element_blocks),
        "leaf",
        split_axis=0,
        concat_axis=0,
        tiled=True,
    )
    return (owned_density, diag_density)


def solution(mesh):
    placed = (
        P("pole", None, "leaf", None),
        P("pole", "leaf", None),
        P("pole", None, None),
        P("pole", None),
        P(),
        P("leaf", None),
    )
    return jax.shard_map(
        body, mesh=mesh, in_specs=placed, out_specs=(P("leaf", None, None), P()), check_vma=False
    )
```

profile of v0, /device:TPU:1, one launch (start us, length us, event | category | flops | bytes accessed | tf_op | source)
XLA Modules:
  0.0 519.0 jit_solution(18408811787066555844)
XLA Ops:
  7.2 0.7 all-gather.2.cloned.1.call-update
  8.0 0.7 select_reduce_fusion.1
  8.7 0.9 select_reduce_fusion
  9.6 1.1 convert_multiply_fusion
  10.7 105.5 %all-gather.2.cloned.1.call-done = bf16[1,8192,512]{2,1,0:T(8,128)(2,1)} async-done(((bf16[1,256,512]{2,1,0:T(8,128)(2,1)}), bf16[1,8192,512]{2,1,0:T(8,128)(2,1)}) %all-gather.2.cloned.1.call-update) | async-done | bytes 8388624 | tf_op jit(solution)/shard_map/all_gather | solution.py:23
  116.2 10.4 %fusion.5 = f32[1,2,256,512]{3,2,1,0:T(8,128)S(1)} fusion(bf16[1,2,256,8192]{3,2,1,0:T(8,128)(2,1)} %param.6, bf16[1,8192,512]{2,1,0:T(8,128)(2,1)} %all-gather.2.cloned.1.call-done, bf16[8192]{0:T(1024)(128)(2,1)S(1)} %convert_convert_fusion), kind=kOutput, calls=%fused_computation.6 | convolution fusion | flops 4311744512 | bytes 17842176 | tf_op jit(solution)/shard_map/pcrk,pkn->pcrn/dot_general | solution.py:15
  126.6 0.7 fusion.18
  127.2 0.7 fusion.22
  127.9 1.4 fusion.10
  129.3 1.4 fusion.11
  130.7 0.0 all-reduce.7.cloned.1.call-start
  130.8 0.1 convert_element_type.34
  130.8 0.6 fusion.41
  131.4 2.0 fusion.26
  133.4 262.7 %all-reduce.5.cloned.1.call-done = (f32[1,256,256]{2,1,0:T(8,128)}, f32[1,256,256]{2,1,0:T(8,128)}) async-done(((f32[1,256,256]{2,1,0:T(8,128)}, f32[1,256,256]{2,1,0:T(8,128)}), (f32[1,256,256]{2,1,0:T(8,128)}, f32[1,256,256]{2,1,0:T(8,128)})) %all-reduce.5.cloned.1.call-update) | async-done | bytes 524304 | tf_op jit(solution)/shard_map/psum | solution.py:45
  396.1 3.0 fusion.14
  399.2 0.1 fusion.35
  399.3 0.1 reduce_window_sum.11
  399.3 0.2 select_reduce_fusion.2
  399.5 74.7 %all-reduce.7.cloned.1.call-done = (f32[32,8,256]{2,1,0:T(8,128)}, f32[256,256]{1,0:T(8,128)}) async-done(((f32[32,8,256]{2,1,0:T(8,128)}, f32[256,256]{1,0:T(8,128)}), (f32[32,8,256]{2,1,0:T(8,128)}, f32[256,256]{1,0:T(8,128)})) %all-reduce.7.cloned.1.call-update) | async-done | bytes 524304 | tf_op jit(solution)/shard_map/psum | solution.py:57
  474.3 2.8 scatter_fusion
  477.1 32.8 %all_to_all.5 = f32[64,8,256]{2,1,0:T(8,128)S(1)} all-to-all(f32[64,8,256]{2,1,0:T(8,128)S(1)} %scatter_fusion), channel_id=1, replica_groups=mesh['pole'=8,'leaf'=32] {'leaf'}, dimensions={0} | all-to-all | bytes 1048576 | tf_op jit(solution)/shard_map/all_to_all | solution.py:61
  510.0 0.8 copy.14
  510.8 1.7 copy.15
  (16 shorter events, 0.2 us)
Async XLA Ops:
  7.2 109.0 %all-gather.2.cloned.1.call-start = ((), (), s32[]{:S(2)}) async-start(), calls=%async_computation.1 | async-start | bytes 8650752 | tf_op jit(solution)/shard_map/all_gather | solution.py:23
  7.9 388.2 %all-reduce.5.cloned.1.call-start = ((), (), s32[]{:S(2)}) async-start(), calls=%async_computation.2 | async-start | bytes 1048576 | tf_op jit(solution)/shard_map/psum | solution.py:45
  10.7 120.0 %copy-start = (bf16[1,256,512]{2,1,0:T(8,128)(2,1)S(1)}, bf16[1,256,512]{2,1,0:T(8,128)(2,1)}, u32[]{:S(2)}) copy-start(bf16[1,256,512]{2,1,0:T(8,128)(2,1)} %param.8) | copy-start | bytes 786436
  10.7 120.1 %copy-start.2 = (f32[1,2]{1,0:T(1,128)S(1)}, f32[1,2]{1,0:T(1,128)}, u32[]{:S(2)}) copy-start(f32[1,2]{1,0:T(1,128)} %param.9) | copy-start | bytes 28
  10.7 388.4 %copy-start.1 = (s32[32,1]{0,1:T(1,128)S(1)}, s32[32,1]{0,1:T(1,128)}, u32[]{:S(2)}) copy-start(s32[32,1]{0,1:T(1,128)} %param.11) | copy-start | bytes 388
  130.7 343.5 %all-reduce.7.cloned.1.call-start = ((), (), s32[]{:S(2)}) async-start(), calls=%async_computation.3 | async-start | bytes 1048576 | tf_op jit(solution)/shard_map/psum | solution.py:57
Sparse Core Ops, SparseCore 0:
  10.7 105.4 all-gather.1
  130.8 265.2 all-reduce.4
  399.4 74.7 all-reduce.6
where the time goes:
time: 519 us
  waiting for transfers between devices  444 us (86%)
  blocking collectives  32.8 us (6%)
  matrix products  14.4 us (3%)
  between operations  13.9 us (3%)
  other arithmetic  8.1 us (2%)
  local copies, waits for them, and re-layouts  5.93 us (1%)
    psum x1, waiting for transfers between devices, body(): schur_real, schur_imag = lax.psum((schur_real, schur_imag), 'leaf')  263 us
    all_gather x1, waiting for transfers between devices, body(): panel_rows = lax.all_gather(factor_panel, 'leaf', axis=1, tiled=True)  105 us
    psum x1, waiting for transfers between devices, body(): density_rows = lax.psum(density_part, 'pole')  74.7 us
    all_to_all x1, blocking collectives, body(): lax.all_to_all(buffer_zero.at[slot_index].set(element_blocks), 'leaf', sp...  32.8 us
  transfers between devices with their start and end apart: 3, of which 3 were waited for; matrix products, arithmetic and copies ran while one was open for 1% of the time, Pallas kernels for 0%

commit v1 on v0

--- a/solution.py
+++ b/solution.py
@@ -2,6 +2,11 @@
 import jax.numpy as jnp
 from jax import lax
 from jax.sharding import PartitionSpec as P
+
+
+def stack_and_merge(value, mesh_axis, d):
+    blocks = lax.all_gather(value, mesh_axis)
+    return jnp.concatenate(blocks, axis=d)
 
 
 def kept_rows(structure, first_row, row_count, block_width):
@@ -20,7 +25,7 @@
     rows_here = inverse_front.shape[2]
     block_width = factor_panel.shape[2] // 2
     first_row = lax.axis_index("leaf") * rows_here
-    panel_rows = lax.all_gather(factor_panel, "leaf", axis=1, tiled=True)
+    panel_rows = stack_and_merge(factor_panel, "leaf", 1)
     row_count = panel_rows.shape[1]
     keep_piece = kept_rows(structure, jnp.int32(0), row_count, block_width).astype(jnp.bfloat16)
     masked = panel_rows * keep_piece[None, :, None]

time: 519 us -> 521 us (level)
  no operation moved by 1% of the time
where the time goes in v1:
time: 521 us
  waiting for transfers between devices  444 us (85%)
  blocking collectives  32.8 us (6%)
  between operations  13.9 us (3%)
  other arithmetic  12.8 us (2%)
  matrix products  11.1 us (2%)
  local copies, waits for them, and re-layouts  5.94 us (1%)
    psum x1, waiting for transfers between devices, body(): schur_real, schur_imag = lax.psum((schur_real, schur_imag), 'leaf')  263 us
    all_gather x1, waiting for transfers between devices, stack_and_merge(): blocks = lax.all_gather(value, mesh_axis)  105 us
    psum x1, waiting for transfers between devices, body(): density_rows = lax.psum(density_part, 'pole')  74.7 us
    all_to_all x1, blocking collectives, body(): lax.all_to_all(buffer_zero.at[slot_index].set(element_blocks), 'leaf', sp...  32.8 us
  transfers between devices with their start and end apart: 3, of which 3 were waited for; matrix products, arithmetic and copies ran while one was open for 1% of the time, Pallas kernels for 0%

profile of v1, /device:TPU:1, one launch (start us, length us, event | category | flops | bytes accessed | tf_op | source)
XLA Modules:
  0.0 520.8 jit_solution(2770347157786636679)
XLA Ops:
  7.2 0.7 all-gather.3.cloned.1.call-update
  8.0 0.7 select_reduce_fusion.1
  8.7 0.9 select_reduce_fusion
  9.7 1.1 convert_multiply_fusion
  10.7 105.5 %all-gather.3.cloned.1.call-done = bf16[32,256,512]{2,1,0:T(8,128)(2,1)} async-done(((bf16[1,256,512]{2,1,0:T(8,128)(2,1)}), bf16[32,256,512]{2,1,0:T(8,128)(2,1)}) %all-gather.3.cloned.1.call-update) | async-done | bytes 8388624 | tf_op jit(solution)/shard_map/all_gather | solution.py:8
  116.2 4.7 bitcast_multiply_fusion
  120.9 7.0 %fusion.2 = f32[1,2,256,512]{3,2,1,0:T(8,128)S(1)} fusion(bf16[8192,512,1]{1,0,2:T(8,128)(2,1)S(1)} %bitcast.81, bf16[1,2,256,8192]{3,2,1,0:T(8,128)(2,1)} %param.6), kind=kOutput, calls=%fused_computation.4 | convolution fusion | flops 4294967296 | bytes 17825792 | tf_op jit(solution)/shard_map/pcrk,pkn->pcrn/dot_general | solution.py:20
  128.0 0.7 fusion.13
  128.6 0.7 fusion.17
  129.3 1.4 fusion.5
  130.7 1.4 fusion.6
  132.1 0.1 convert_element_type.39
  132.2 0.6 fusion.36
  132.8 2.0 fusion.21
  134.8 263.2 %all-reduce.5.cloned.1.call-done = (f32[1,256,256]{2,1,0:T(8,128)}, f32[1,256,256]{2,1,0:T(8,128)}) async-done(((f32[1,256,256]{2,1,0:T(8,128)}, f32[1,256,256]{2,1,0:T(8,128)}), (f32[1,256,256]{2,1,0:T(8,128)}, f32[1,256,256]{2,1,0:T(8,128)})) %all-reduce.5.cloned.1.call-update) | async-done | bytes 524304 | tf_op jit(solution)/shard_map/psum | solution.py:50
  398.0 3.0 fusion.9
  401.0 0.1 fusion.30
  401.1 0.1 reduce_window_sum.11
  401.1 0.2 select_reduce_fusion.2
  401.3 74.7 %all-reduce.7.cloned.1.call-done = (f32[32,8,256]{2,1,0:T(8,128)}, f32[256,256]{1,0:T(8,128)}) async-done(((f32[32,8,256]{2,1,0:T(8,128)}, f32[256,256]{1,0:T(8,128)}), (f32[32,8,256]{2,1,0:T(8,128)}, f32[256,256]{1,0:T(8,128)})) %all-reduce.7.cloned.1.call-update) | async-done | bytes 524304 | tf_op jit(solution)/shard_map/psum | solution.py:62
  476.1 2.8 scatter_fusion
  478.9 32.8 %all_to_all.5 = f32[64,8,256]{2,1,0:T(8,128)S(1)} all-to-all(f32[64,8,256]{2,1,0:T(8,128)S(1)} %scatter_fusion), channel_id=1, replica_groups=mesh['pole'=8,'leaf'=32] {'leaf'}, dimensions={0} | all-to-all | bytes 1048576 | tf_op jit(solution)/shard_map/all_to_all | solution.py:66
  511.8 0.8 copy.14
  512.6 1.7 copy.15
  (18 shorter events, 0.3 us)
Async XLA Ops:
  7.2 109.0 %all-gather.3.cloned.1.call-start = ((), (), s32[]{:S(2)}) async-start(), calls=%async_computation.1 | async-start | bytes 8650752 | tf_op jit(solution)/shard_map/all_gather | solution.py:8
  7.9 390.1 %all-reduce.5.cloned.1.call-start = ((), (), s32[]{:S(2)}) async-start(), calls=%async_computation.2 | async-start | bytes 1048576 | tf_op jit(solution)/shard_map/psum | solution.py:50
  120.9 11.3 %copy-start = (bf16[1,256,512]{2,1,0:T(8,128)(2,1)S(1)}, bf16[1,256,512]{2,1,0:T(8,128)(2,1)}, u32[]{:S(2)}) copy-start(bf16[1,256,512]{2,1,0:T(8,128)(2,1)} %param.8) | copy-start | bytes 786436
  120.9 11.3 %copy-start.2 = (f32[1,2]{1,0:T(1,128)S(1)}, f32[1,2]{1,0:T(1,128)}, u32[]{:S(2)}) copy-start(f32[1,2]{1,0:T(1,128)} %param.9) | copy-start | bytes 28
  120.9 280.1 %copy-start.1 = (s32[32,1]{0,1:T(1,128)S(1)}, s32[32,1]{0,1:T(1,128)}, u32[]{:S(2)}) copy-start(s32[32,1]{0,1:T(1,128)} %param.11) | copy-start | bytes 388
  132.1 344.0 %all-reduce.7.cloned.1.call-start = ((), (), s32[]{:S(2)}) async-start(), calls=%async_computation.3 | async-start | bytes 1048576 | tf_op jit(solution)/shard_map/psum | solution.py:62
Sparse Core Ops, SparseCore 0:
  10.7 105.4 all-gather.2
  132.2 265.7 all-reduce.4
  401.2 74.7 all-reduce.6
